TPU v7x, 512 devices: a whole 4x8x8 slice. The times are simulated.
512 devices in a mesh: row: 16 (over y, core), col: 32 (over z, x).
Axes of the slice: x: 4, y: 8, z: 8, core: 2. Of those that a mesh axis runs over, the one named last changes fastest.
Arguments:
- surface: float32 [2, 1024, 4096], P(None, 'row', 'col'), may hold values from -0.5 to 0.5
- u_face: float32 [2, 1024, 4096], P(None, 'row', 'col'), may hold values from -3 to 3
- v_face: float32 [2, 1024, 4096], P(None, 'row', 'col'), may hold values from -3 to 3
- bed_depth: float32 [1024, 4096], P('row', 'col'), may hold values from 1 to 10
- wet_mask: int32 [2, 1024, 4096], P(None, 'row', 'col'), may hold values 0 or 1
- rainfall: float32 [2, 1024, 4096], P(None, 'row', 'col'), may hold values from 0.05 to 0.5
Outputs:
- new_surface: float32 [2, 1024, 4096], P(None, 'row', 'col')
- new_u: float32 [2, 1024, 4096], P(None, 'row', 'col')
- new_v: float32 [2, 1024, 4096], P(None, 'row', 'col')
All inputs are finite; a program needn't handle non-finite values. No bound on the sum of `wet_mask` on one device may be relied on, other than what follows from the above.
Results may differ from a plain program's by a relative error of at most 0.0003.
Values sent between devices are 32-bit elements; how exact they have to be, the bound alone decides.
A program may use at most 64 MiB of HBM per device.

v0:
```python
import jax
import jax.numpy as jnp
from jax import lax
from jax.sharding import PartitionSpec as P

ITERS = 3
DTDX = 0.5
FRIC = 0.05
G1 = 4.0
CK = DTDX * G1


def extended(cells, sides, width):
    for axis, dim in sides:
        count = lax.axis_size(axis)
        ends = count - 1
        head = lax.slice_in_dim(cells, 0, width, axis=dim)
        tail = lax.slice_in_dim(cells, cells.shape[dim] - width, cells.shape[dim], axis=dim)
        cells = jnp.concatenate(
            [
                lax.ppermute(tail, axis, [(i, (i + 1) % count) for i in range(ends)]),
                cells,
                lax.ppermute(head, axis, [((i + 1) % count, i) for i in range(ends)]),
            ],
            axis=dim,
        )
    return cells


def passed_along(block, axis, distance):
    devices = range(lax.axis_size(axis))
    route = [(i - distance, i) for i in devices if i - distance in devices]
    return lax.ppermute(block, axis, route)


def explicit(eta2, u2, v2, dep2, wet2, ny, nx):

    def view(a, dy, dx):
        return a[:, 1 + dy : 3 + dy + ny, 1 + dx : 3 + dx + nx]

    h_here = view(eta2, 0, 0) + view(dep2, 0, 0)
    h_east = view(eta2, 0, 1) + view(dep2, 0, 1)
    h_north = view(eta2, 1, 0) + view(dep2, 1, 0)
    wet_x = view(wet2, 0, 0) * view(wet2, 0, 1)
    wet_y = view(wet2, 0, 0) * view(wet2, 1, 0)
    depth_x = 0.5 * (h_here + h_east)
    depth_y = 0.5 * (h_here + h_north)
    u_here = view(u2, 0, 0)
    v_here = view(v2, 0, 0)
    v_mean = 0.25 * (v_here + view(v2, 0, 1) + view(v2, -1, 0) + view(v2, -1, 1))
    u_mean = 0.25 * (u_here + view(u2, 0, -1) + view(u2, 1, 0) + view(u2, 1, -1))
    adv_u = jnp.where(
        u_here > 0, u_here * (u_here - view(u2, 0, -1)), u_here * (view(u2, 0, 1) - u_here)
    )
    adv_u = adv_u + jnp.where(
        v_mean > 0, v_mean * (u_here - view(u2, -1, 0)), v_mean * (view(u2, 1, 0) - u_here)
    )
    adv_v = jnp.where(
        v_here > 0, v_here * (v_here - view(v2, -1, 0)), v_here * (view(v2, 1, 0) - v_here)
    )
    adv_v = adv_v + jnp.where(
        u_mean > 0, u_mean * (v_here - view(v2, 0, -1)), u_mean * (view(v2, 0, 1) - v_here)
    )
    u_star = wet_x * (u_here - DTDX * adv_u) / (1.0 + FRIC * jnp.abs(u_here))
    v_star = wet_y * (v_here - DTDX * adv_v) / (1.0 + FRIC * jnp.abs(v_here))
    return (
        u_star,
        v_star,
        wet_x,
        wet_y,
        CK * depth_x * wet_x,
        CK * depth_y * wet_y,
        depth_x * u_star,
        depth_y * v_star,
    )


def inner(a):
    return a[:, 1:-1, 1:-1]


def right_side(eta, rain, flux_x, flux_y):
    div = inner(flux_x) - flux_x[:, 1:-1, :-2] + (inner(flux_y) - flux_y[:, :-2, 1:-1])
    return eta + rain - DTDX * div


def operate(e_pad, coef_x, coef_y):
    e_mid = inner(e_pad)
    out = (
        e_mid
        + inner(coef_x) * (e_mid - e_pad[:, 1:-1, 2:])
        + coef_x[:, 1:-1, :-2] * (e_mid - e_pad[:, 1:-1, :-2])
    )
    return (
        out
        + inner(coef_y) * (e_mid - e_pad[:, 2:, 1:-1])
        + coef_y[:, :-2, 1:-1] * (e_mid - e_pad[:, :-2, 1:-1])
    )


def field_pad(field):
    return extended(field, (("row", 1), ("col", 2)), 1)


def squares(residual):
    return lax.psum(jnp.sum(residual * residual, axis=(1, 2)), ("row", "col"))


def spread(values):
    return values[:, None, None]


def body(surface, u_face, v_face, bed_depth, wet_mask, rainfall):
    rows = surface.shape[1]
    cols = surface.shape[2]
    stacked = jnp.stack(
        [
            surface,
            u_face,
            v_face,
            jnp.broadcast_to(bed_depth[None], surface.shape),
            wet_mask.astype(jnp.float32),
        ]
    )
    padded = extended(stacked, (("row", 2), ("col", 3)), 2)
    u_star, v_star, wet_x, wet_y, coef_x, coef_y, flux_x, flux_y = explicit(
        padded[0], padded[1], padded[2], padded[3], padded[4], rows, cols
    )
    rhs = right_side(surface, rainfall, flux_x, flux_y)
    start_pad = padded[0][:, 1:-1, 1:-1]
    solution = surface
    residual = rhs - operate(start_pad, coef_x, coef_y)
    direction = residual
    norm_now = squares(residual)
    for step in range(ITERS):
        direction_pad = field_pad(direction)
        image = operate(direction_pad, coef_x, coef_y)
        alpha = norm_now / lax.psum(jnp.sum(direction * image, axis=(1, 2)), ("row", "col"))
        solution = solution + spread(alpha) * direction
        residual = residual - spread(alpha) * image
        norm_next = squares(residual)
        direction = residual + spread(norm_next / norm_now) * direction
        norm_now = norm_next
    east_col = passed_along(solution[:, :, :1], "col", -1)
    north_row = passed_along(solution[:, :1, :], "row", -1)
    east_field = jnp.concatenate([solution[:, :, 1:], east_col], axis=2)
    north_field = jnp.concatenate([solution[:, 1:, :], north_row], axis=1)
    new_u = inner(u_star) - G1 * inner(wet_x) * (east_field - solution)
    new_v = inner(v_star) - G1 * inner(wet_y) * (north_field - solution)
    return (solution, new_u, new_v)


def solution(mesh):
    in_specs = (
        P(None, "row", "col"),
        P(None, "row", "col"),
        P(None, "row", "col"),
        P("row", "col"),
        P(None, "row", "col"),
        P(None, "row", "col"),
    )
    out_specs = (P(None, "row", "col"), P(None, "row", "col"), P(None, "row", "col"))
    return jax.shard_map(body, mesh=mesh, in_specs=in_specs, out_specs=out_specs, check_vma=False)
```

profile of v0, /device:TPU:14, one launch (start us, length us, event | category | flops | bytes accessed | tf_op | source)
XLA Modules:
  0.0 589.8 jit_solution(1745346275453686401)
XLA Ops:
  4.0 1.9 collective-permute-start
  5.9 3.6 collective-permute-start.1
  11.1 4.2 collective-permute-start.2
  15.3 1.9 collective-permute-start.3
  17.3 6.6 %collective-permute-done.2 = f32[5,2,68,2]{3,2,1,0:T(8,128)S(1)} collective-permute-done((f32[5,2,68,2]{3,2,1,0:T(8,128)S(1)}, f32[5,2,68,2]{3,2,1,0:T(8,128)S(1)}, u32[]{:S(2)}, u32[]{:S(2)}) %collective-permute-start.2) | collective-permute-done | bytes 5472 | tf_op jit(solution)/shard_map/ppermute | solution.py:21
  23.8 6.6 %collective-permute-done.3 = f32[5,2,68,2]{3,2,1,0:T(8,128)S(1)} collective-permute-done((f32[5,2,68,2]{3,2,1,0:T(8,128)S(1)}, f32[5,2,68,2]{3,2,1,0:T(8,128)S(1)}, u32[]{:S(2)}, u32[]{:S(2)}) %collective-permute-start.3) | collective-permute-done | bytes 5472 | tf_op jit(solution)/shard_map/ppermute | solution.py:23
  34.8 2.4 collective-permute-start.4
  37.3 2.5 collective-permute-done.4
  41.7 6.0 %collective-permute-start.7 = (f32[2,66,1]{2,1,0:T(8,128)S(1)}, f32[2,66,1]{2,1,0:T(8,128)S(1)}, u32[]{:S(2)}, u32[]{:S(2)}) collective-permute-start(f32[2,66,1]{2,1,0:T(8,128)S(1)} %get-tuple-element.39), channel_id=1, source_target_pairs={{0,1},{1,2},{2,3},{3,4},{4,5},{5,6},{6,7},{7,8},{8,9},{9,10},{10,1... | collective-permute-start | bytes 1592 | tf_op jit(solution)/shard_map/ppermute | solution.py:21
  50.0 105.9 %all-reduce = (f32[2]{0:T(128)S(1)}, f32[2]{0:T(128)S(1)}) all-reduce(f32[2]{0:T(128)S(1)} %get-tuple-element.4, f32[2]{0:T(128)S(1)} %get-tuple-element.3), channel_id=1, replica_groups=mesh['row'=16,'col'=32] {'row','col'}, use_global_device_ids=true, to_apply=%region_1.2 | all-reduce | flops 4 | bytes 32 | tf_op jit(solution)/shard_map/psum | solution.py:106
  156.1 94.5 %psum.44 = f32[2]{0:T(128)S(1)} all-reduce(f32[2]{0:T(128)S(1)} %get-tuple-element.9), channel_id=1, replica_groups=mesh['row'=16,'col'=32] {'row','col'}, use_global_device_ids=true, to_apply=%region_5.6 | all-reduce | flops 2 | bytes 16 | tf_op jit(solution)/shard_map/psum | solution.py:106
  252.6 2.4 collective-permute-start.8
  255.1 2.5 collective-permute-done.8
  257.6 2.2 collective-permute-start.10
  259.8 5.8 collective-permute-start.11
  267.8 99.5 %psum.45 = f32[2]{0:T(128)S(1)} all-reduce(f32[2]{0:T(128)S(1)} %get-tuple-element.7), channel_id=1, replica_groups=mesh['row'=16,'col'=32] {'row','col'}, use_global_device_ids=true, to_apply=%region_7.8 | all-reduce | flops 2 | bytes 16 | tf_op jit(solution)/shard_map/psum | solution.py:138
  367.5 94.4 %psum.46 = f32[2]{0:T(128)S(1)} all-reduce(f32[2]{0:T(128)S(1)} %multiply_reduce_fusion), channel_id=1, replica_groups=mesh['row'=16,'col'=32] {'row','col'}, use_global_device_ids=true, to_apply=%region_9.10 | all-reduce | flops 2 | bytes 16 | tf_op jit(solution)/shard_map/psum | solution.py:106
  461.9 1.9 collective-permute-start.13
  463.9 2.4 collective-permute-start.12
  466.3 2.5 collective-permute-done.12
  468.8 2.2 collective-permute-start.14
  471.1 5.7 collective-permute-start.15
  479.0 99.4 %psum.47 = f32[2]{0:T(128)S(1)} all-reduce(f32[2]{0:T(128)S(1)} %fusion.28), channel_id=1, replica_groups=mesh['row'=16,'col'=32] {'row','col'}, use_global_device_ids=true, to_apply=%region_11.12 | all-reduce | flops 2 | bytes 16 | tf_op jit(solution)/shard_map/psum | solution.py:138
  582.5 6.5 %collective-permute-done.16 = f32[2,64,1]{2,1,0:T(8,128)S(1)} collective-permute-done((f32[2,64,1]{2,1,0:T(8,128)S(1)}, f32[2,64,1]{2,1,0:T(8,128)S(1)}, u32[]{:S(2)}, u32[]{:S(2)}) %collective-permute-start.16) | collective-permute-done | bytes 544 | tf_op jit(solution)/shard_map/ppermute | solution.py:33
  (71 shorter events, 25.4 us)
Async XLA Ops:
  0.6 0.9 copy-start.3
  1.5 0.8 copy-start.4
  3.1 0.8 copy-start.5
  4.0 5.6 collective-permute-start
  5.9 5.0 collective-permute-start.1
  11.1 12.7 %collective-permute-start.2 = (f32[5,2,68,2]{3,2,1,0:T(8,128)S(1)}, f32[5,2,68,2]{3,2,1,0:T(8,128)S(1)}, u32[]{:S(2)}, u32[]{:S(2)}) collective-permute-start(f32[5,2,68,2]{3,2,1,0:T(8,128)S(1)} %get-tuple-element.30), channel_id=1, source_target_pairs={{0,1},{1,2},{2,3},{3,4},{4,5},{5,6},{6,7},{7,8},{8,9},{9,10},{10,1... | collective-permute-start | bytes 16328 | tf_op jit(solution)/shard_map/ppermute | solution.py:21
  15.3 15.1 %collective-permute-start.3 = (f32[5,2,68,2]{3,2,1,0:T(8,128)S(1)}, f32[5,2,68,2]{3,2,1,0:T(8,128)S(1)}, u32[]{:S(2)}, u32[]{:S(2)}) collective-permute-start(f32[5,2,68,2]{3,2,1,0:T(8,128)S(1)} %get-tuple-element.31), channel_id=1, source_target_pairs={{1,0},{2,1},{3,2},{4,3},{5,4},{6,5},{7,6},{8,7},{9,8},{10,9},{11,1... | collective-permute-start | bytes 16328 | tf_op jit(solution)/shard_map/ppermute | solution.py:23
  31.8 0.8 copy-start.1
  31.8 0.9 copy-start.2
  32.9 4.3 collective-permute-start.5
  34.8 4.9 collective-permute-start.4
  39.8 8.4 %collective-permute-start.6 = (f32[2,66,1]{2,1,0:T(8,128)S(1)}, f32[2,66,1]{2,1,0:T(8,128)S(1)}, u32[]{:S(2)}, u32[]{:S(2)}) collective-permute-start(f32[2,66,1]{2,1,0:T(8,128)S(1)} %get-tuple-element.38), channel_id=1, source_target_pairs={{1,0},{2,1},{3,2},{4,3},{5,4},{6,5},{7,6},{8,7},{9,8},{10,9},{11,1... | collective-permute-start | bytes 1592 | tf_op jit(solution)/shard_map/ppermute | solution.py:23
  41.7 8.0 %collective-permute-start.7 = (f32[2,66,1]{2,1,0:T(8,128)S(1)}, f32[2,66,1]{2,1,0:T(8,128)S(1)}, u32[]{:S(2)}, u32[]{:S(2)}) collective-permute-start(f32[2,66,1]{2,1,0:T(8,128)S(1)} %get-tuple-element.39), channel_id=1, source_target_pairs={{0,1},{1,2},{2,3},{3,4},{4,5},{5,6},{6,7},{7,8},{8,9},{9,10},{10,1... | collective-permute-start | bytes 1592 | tf_op jit(solution)/shard_map/ppermute | solution.py:21
  250.7 4.3 collective-permute-start.9
  252.6 4.9 collective-permute-start.8
  257.6 8.4 %collective-permute-start.10 = (f32[2,66,1]{2,1,0:T(8,128)S(1)}, f32[2,66,1]{2,1,0:T(8,128)S(1)}, u32[]{:S(2)}, u32[]{:S(2)}) collective-permute-start(f32[2,66,1]{2,1,0:T(8,128)S(1)} %get-tuple-element.36), channel_id=1, source_target_pairs={{1,0},{2,1},{3,2},{4,3},{5,4},{6,5},{7,6},{8,7},{9,8},{10,9},{11,1... | collective-permute-start | bytes 1592 | tf_op jit(solution)/shard_map/ppermute | solution.py:23
  259.8 7.7 %collective-permute-start.11 = (f32[2,66,1]{2,1,0:T(8,128)S(1)}, f32[2,66,1]{2,1,0:T(8,128)S(1)}, u32[]{:S(2)}, u32[]{:S(2)}) collective-permute-start(f32[2,66,1]{2,1,0:T(8,128)S(1)} %get-tuple-element.37), channel_id=1, source_target_pairs={{0,1},{1,2},{2,3},{3,4},{4,5},{5,6},{6,7},{7,8},{8,9},{9,10},{10,1... | collective-permute-start | bytes 1592 | tf_op jit(solution)/shard_map/ppermute | solution.py:21
  461.9 4.3 collective-permute-start.13
  463.9 4.9 collective-permute-start.12
  468.8 8.4 %collective-permute-start.14 = (f32[2,66,1]{2,1,0:T(8,128)S(1)}, f32[2,66,1]{2,1,0:T(8,128)S(1)}, u32[]{:S(2)}, u32[]{:S(2)}) collective-permute-start(f32[2,66,1]{2,1,0:T(8,128)S(1)} %get-tuple-element.34), channel_id=1, source_target_pairs={{1,0},{2,1},{3,2},{4,3},{5,4},{6,5},{7,6},{8,7},{9,8},{10,9},{11,1... | collective-permute-start | bytes 1592 | tf_op jit(solution)/shard_map/ppermute | solution.py:23
  471.1 7.7 %collective-permute-start.15 = (f32[2,66,1]{2,1,0:T(8,128)S(1)}, f32[2,66,1]{2,1,0:T(8,128)S(1)}, u32[]{:S(2)}, u32[]{:S(2)}) collective-permute-start(f32[2,66,1]{2,1,0:T(8,128)S(1)} %get-tuple-element.35), channel_id=1, source_target_pairs={{0,1},{1,2},{2,3},{3,4},{4,5},{5,6},{6,7},{7,8},{8,9},{9,10},{10,1... | collective-permute-start | bytes 1592 | tf_op jit(solution)/shard_map/ppermute | solution.py:21
  578.5 10.5 %copy-start = (f32[2,64,128]{2,1,0:T(8,128)}, f32[2,64,128]{2,1,0:T(8,128)S(1)}, u32[]{:S(2)}) copy-start(f32[2,64,128]{2,1,0:T(8,128)S(1)} %multiply_add_fusion) | copy-start | bytes 196612
  578.5 10.4 %collective-permute-start.17 = (f32[2,1,128]{2,1,0:T(1,128)S(1)}, f32[2,1,128]{2,1,0:T(1,128)S(1)}, u32[]{:S(2)}, u32[]{:S(2)}) collective-permute-start(f32[2,1,128]{2,1,0:T(1,128)S(1)} %slice.398), channel_id=1, source_target_pairs={{32,0},{64,32},{96,64},{128,96},{160,128},{192,160},{224,192},{256... | collective-permute-start | bytes 3080 | tf_op jit(solution)/shard_map/ppermute | solution.py:33
  580.5 8.5 %collective-permute-start.16 = (f32[2,64,1]{2,1,0:T(8,128)S(1)}, f32[2,64,1]{2,1,0:T(8,128)S(1)}, u32[]{:S(2)}, u32[]{:S(2)}) collective-permute-start(f32[2,64,1]{2,1,0:T(8,128)S(1)} %bitcast.19), channel_id=1, source_target_pairs={{1,0},{2,1},{3,2},{4,3},{5,4},{6,5},{7,6},{8,7},{9,8},{10,9},{11,1... | collective-permute-start | bytes 1544 | tf_op jit(solution)/shard_map/ppermute | solution.py:33
  (1 other events, 0.8 us)
where the time goes:
time: 591 us; the launch traced here: 590 us
  blocking collectives  494 us (84%)
  starting transfers between devices  52.3 us (9%)
  waiting for transfers between devices  34.3 us (6%)
    psum x3, blocking collectives, squares(): return lax.psum(jnp.sum(residual * residual, axis=(1, 2)), ('row', 'col'))  295 us
    psum x2, blocking collectives, body(): lax.psum(jnp.sum(direction * image, axis=(1, 2)), ('row', 'col'))  199 us
    ppermute x8, starting transfers between devices, extended(): lax.ppermute(tail, axis, [(i, (i + 1) % count) for i in range(ends)])  30.9 us
    ppermute x8, waiting for transfers between devices, extended(): lax.ppermute(tail, axis, [(i, (i + 1) % count) for i in range(ends)])  18.7 us
    ppermute x8, starting transfers between devices, extended(): lax.ppermute(head, axis, [((i + 1) % count, i) for i in range(ends)])  17.6 us
  transfers between devices with their start and end apart: 18, of which 13 were waited for; matrix products, arithmetic and copies ran while one was open for 0% of the time, Pallas kernels for 0%

commit v1 on v0

--- a/solution.py
+++ b/solution.py
@@ -103,7 +103,7 @@
 
 
 def squares(residual):
-    return lax.psum(jnp.sum(residual * residual, axis=(1, 2)), ("row", "col"))
+    return lax.psum(lax.psum(jnp.sum(residual * residual, axis=(1, 2)), "row"), "col")
 
 
 def spread(values):

time: 591 us -> 683 us (1.16)
  blocking collectives: 494 us -> 579 us
    psum x2 -> x3, blocking collectives: 199 us -> 309 us  [body(): lax.psum(jnp.sum(direction * image, axis=(1, 2)), ('row', 'col'))]
    psum x3 -> x6, blocking collectives: 295 us -> 270 us  [the longest x3 206 us: squares(): lax.psum(lax.psum(jnp.sum(residual * residual, axis=(1, 2)), 'row'), 'col')]
where the time goes in v1:
time: 683 us; the launch traced here: 682 us
  blocking collectives  579 us (85%)
  starting transfers between devices  52.3 us (8%)
  waiting for transfers between devices  41.1 us (6%)
    psum x3, blocking collectives, body(): lax.psum(jnp.sum(direction * image, axis=(1, 2)), ('row', 'col'))  309 us
    psum x3, blocking collectives, squares(): lax.psum(lax.psum(jnp.sum(residual * residual, axis=(1, 2)), 'row'), 'col')  206 us
    psum x3, blocking collectives, squares(): lax.psum(jnp.sum(residual * residual, axis=(1, 2)), 'row')  64.5 us
    ppermute x8, starting transfers between devices, extended(): lax.ppermute(tail, axis, [(i, (i + 1) % count) for i in range(ends)])  29.4 us
    ppermute x8, waiting for transfers between devices, extended(): lax.ppermute(tail, axis, [(i, (i + 1) % count) for i in range(ends)])  25.5 us
    ppermute x8, starting transfers between devices, extended(): lax.ppermute(head, axis, [((i + 1) % count, i) for i in range(ends)])  19.2 us
  transfers between devices with their start and end apart: 18, of which 13 were waited for; matrix products, arithmetic and copies ran while one was open for 0% of the time, Pallas kernels for 0%

profile of v1, /device:TPU:14, one launch (start us, length us, event | category | flops | bytes accessed | tf_op | source)
XLA Modules:
  0.0 682.1 jit_solution(3120193788076422963)
XLA Ops:
  5.9 3.6 collective-permute-start.1
  11.1 4.2 collective-permute-start.2
  17.3 6.6 collective-permute-done.2
  23.8 6.6 collective-permute-done.3
  34.8 2.4 collective-permute-start.4
  37.3 2.5 collective-permute-done.4
  41.7 6.0 collective-permute-start.7
  50.0 21.1 %psum.63 = f32[2]{0:T(128)S(1)} all-reduce(f32[2]{0:T(128)S(1)} %get-tuple-element.4), channel_id=1, replica_groups=mesh['row'=16,'col'=32] {'row'}, use_global_device_ids=true, to_apply=%region_1.2 | all-reduce | flops 2 | bytes 16 | tf_op jit(solution)/shard_map/psum | solution.py:106
  71.1 108.7 %psum.65 = f32[2]{0:T(128)S(1)} all-reduce(f32[2]{0:T(128)S(1)} %get-tuple-element.3), channel_id=1, replica_groups=mesh['row'=16,'col'=32] {'row','col'}, use_global_device_ids=true, to_apply=%region_4.5 | all-reduce | flops 2 | bytes 16 | tf_op jit(solution)/shard_map/psum | solution.py:138
  179.8 66.8 %psum.64 = f32[2]{0:T(128)S(1)} all-reduce(f32[2]{0:T(128)S(1)} %psum.63), channel_id=1, replica_groups=mesh['row'=16,'col'=32] {'col'}, use_global_device_ids=true, to_apply=%region_2.3 | all-reduce | flops 2 | bytes 16 | tf_op jit(solution)/shard_map/psum | solution.py:106
  246.8 21.4 %psum.66 = f32[2]{0:T(128)S(1)} all-reduce(f32[2]{0:T(128)S(1)} %get-tuple-element.7), channel_id=1, replica_groups=mesh['row'=16,'col'=32] {'row'}, use_global_device_ids=true, to_apply=%region_6.7 | all-reduce | flops 2 | bytes 16 | tf_op jit(solution)/shard_map/psum | solution.py:106
  268.3 71.9 %psum.67 = f32[2]{0:T(128)S(1)} all-reduce(f32[2]{0:T(128)S(1)} %psum.66), channel_id=1, replica_groups=mesh['row'=16,'col'=32] {'col'}, use_global_device_ids=true, to_apply=%region_7.8 | all-reduce | flops 2 | bytes 16 | tf_op jit(solution)/shard_map/psum | solution.py:106
  344.6 4.3 collective-permute-done.8
  351.0 6.0 collective-permute-start.11
  357.4 3.1 collective-permute-done.11
  360.8 100.1 %psum.68 = f32[2]{0:T(128)S(1)} all-reduce(f32[2]{0:T(128)S(1)} %get-tuple-element.5), channel_id=1, replica_groups=mesh['row'=16,'col'=32] {'row','col'}, use_global_device_ids=true, to_apply=%region_9.10 | all-reduce | flops 2 | bytes 16 | tf_op jit(solution)/shard_map/psum | solution.py:138
  461.1 21.9 %psum.69 = f32[2]{0:T(128)S(1)} all-reduce(f32[2]{0:T(128)S(1)} %multiply_reduce_fusion), channel_id=1, replica_groups=mesh['row'=16,'col'=32] {'row'}, use_global_device_ids=true, to_apply=%region_11.12 | all-reduce | flops 2 | bytes 16 | tf_op jit(solution)/shard_map/psum | solution.py:106
  483.0 66.8 %psum.70 = f32[2]{0:T(128)S(1)} all-reduce(f32[2]{0:T(128)S(1)} %psum.69), channel_id=1, replica_groups=mesh['row'=16,'col'=32] {'col'}, use_global_device_ids=true, to_apply=%region_12.13 | all-reduce | flops 2 | bytes 16 | tf_op jit(solution)/shard_map/psum | solution.py:106
  554.3 4.3 collective-permute-done.12
  558.7 4.0 collective-permute-start.14
  562.7 4.0 collective-permute-start.15
  567.1 3.1 collective-permute-done.15
  570.5 100.2 %psum.71 = f32[2]{0:T(128)S(1)} all-reduce(f32[2]{0:T(128)S(1)} %fusion.28), channel_id=1, replica_groups=mesh['row'=16,'col'=32] {'row','col'}, use_global_device_ids=true, to_apply=%region_14.15 | all-reduce | flops 2 | bytes 16 | tf_op jit(solution)/shard_map/psum | solution.py:138
  674.8 6.5 collective-permute-done.16
  (75 shorter events, 34.7 us)
Async XLA Ops:
  0.6 0.9 copy-start.3
  1.5 0.8 copy-start.4
  3.1 0.8 copy-start.5
  4.0 5.6 collective-permute-start
  5.9 5.0 collective-permute-start.1
  11.1 12.7 %collective-permute-start.2 = (f32[5,2,68,2]{3,2,1,0:T(8,128)S(1)}, f32[5,2,68,2]{3,2,1,0:T(8,128)S(1)}, u32[]{:S(2)}, u32[]{:S(2)}) collective-permute-start(f32[5,2,68,2]{3,2,1,0:T(8,128)S(1)} %get-tuple-element.28), channel_id=1, source_target_pairs={{0,1},{1,2},{2,3},{3,4},{4,5},{5,6},{6,7},{7,8},{8,9},{9,10},{10,1... | collective-permute-start | bytes 16328 | tf_op jit(solution)/shard_map/ppermute | solution.py:21
  15.3 15.1 %collective-permute-start.3 = (f32[5,2,68,2]{3,2,1,0:T(8,128)S(1)}, f32[5,2,68,2]{3,2,1,0:T(8,128)S(1)}, u32[]{:S(2)}, u32[]{:S(2)}) collective-permute-start(f32[5,2,68,2]{3,2,1,0:T(8,128)S(1)} %get-tuple-element.29), channel_id=1, source_target_pairs={{1,0},{2,1},{3,2},{4,3},{5,4},{6,5},{7,6},{8,7},{9,8},{10,9},{11,1... | collective-permute-start | bytes 16328 | tf_op jit(solution)/shard_map/ppermute | solution.py:23
  31.8 0.8 copy-start.1
  31.8 0.9 copy-start.2
  32.9 4.3 collective-permute-start.5
  34.8 4.9 collective-permute-start.4
  39.8 8.4 %collective-permute-start.6 = (f32[2,66,1]{2,1,0:T(8,128)S(1)}, f32[2,66,1]{2,1,0:T(8,128)S(1)}, u32[]{:S(2)}, u32[]{:S(2)}) collective-permute-start(f32[2,66,1]{2,1,0:T(8,128)S(1)} %get-tuple-element.36), channel_id=1, source_target_pairs={{1,0},{2,1},{3,2},{4,3},{5,4},{6,5},{7,6},{8,7},{9,8},{10,9},{11,1... | collective-permute-start | bytes 1592 | tf_op jit(solution)/shard_map/ppermute | solution.py:23
  41.7 8.0 %collective-permute-start.7 = (f32[2,66,1]{2,1,0:T(8,128)S(1)}, f32[2,66,1]{2,1,0:T(8,128)S(1)}, u32[]{:S(2)}, u32[]{:S(2)}) collective-permute-start(f32[2,66,1]{2,1,0:T(8,128)S(1)} %get-tuple-element.37), channel_id=1, source_target_pairs={{0,1},{1,2},{2,3},{3,4},{4,5},{5,6},{6,7},{7,8},{8,9},{9,10},{10,1... | collective-permute-start | bytes 1592 | tf_op jit(solution)/shard_map/ppermute | solution.py:21
  340.3 4.3 collective-permute-start.9
  342.2 6.7 collective-permute-start.8
  349.0 8.4 %collective-permute-start.10 = (f32[2,66,1]{2,1,0:T(8,128)S(1)}, f32[2,66,1]{2,1,0:T(8,128)S(1)}, u32[]{:S(2)}, u32[]{:S(2)}) collective-permute-start(f32[2,66,1]{2,1,0:T(8,128)S(1)} %get-tuple-element.34), channel_id=1, source_target_pairs={{1,0},{2,1},{3,2},{4,3},{5,4},{6,5},{7,6},{8,7},{9,8},{10,9},{11,1... | collective-permute-start | bytes 1592 | tf_op jit(solution)/shard_map/ppermute | solution.py:23
  351.0 9.6 %collective-permute-start.11 = (f32[2,66,1]{2,1,0:T(8,128)S(1)}, f32[2,66,1]{2,1,0:T(8,128)S(1)}, u32[]{:S(2)}, u32[]{:S(2)}) collective-permute-start(f32[2,66,1]{2,1,0:T(8,128)S(1)} %get-tuple-element.35), channel_id=1, source_target_pairs={{0,1},{1,2},{2,3},{3,4},{4,5},{5,6},{6,7},{7,8},{8,9},{9,10},{10,1... | collective-permute-start | bytes 1592 | tf_op jit(solution)/shard_map/ppermute | solution.py:21
  549.9 4.3 collective-permute-start.13
  551.9 6.7 collective-permute-start.12
  558.7 8.4 %collective-permute-start.14 = (f32[2,66,1]{2,1,0:T(8,128)S(1)}, f32[2,66,1]{2,1,0:T(8,128)S(1)}, u32[]{:S(2)}, u32[]{:S(2)}) collective-permute-start(f32[2,66,1]{2,1,0:T(8,128)S(1)} %get-tuple-element.32), channel_id=1, source_target_pairs={{1,0},{2,1},{3,2},{4,3},{5,4},{6,5},{7,6},{8,7},{9,8},{10,9},{11,1... | collective-permute-start | bytes 1592 | tf_op jit(solution)/shard_map/ppermute | solution.py:23
  562.7 7.5 %collective-permute-start.15 = (f32[2,66,1]{2,1,0:T(8,128)S(1)}, f32[2,66,1]{2,1,0:T(8,128)S(1)}, u32[]{:S(2)}, u32[]{:S(2)}) collective-permute-start(f32[2,66,1]{2,1,0:T(8,128)S(1)} %get-tuple-element.33), channel_id=1, source_target_pairs={{0,1},{1,2},{2,3},{3,4},{4,5},{5,6},{6,7},{7,8},{8,9},{9,10},{10,1... | collective-permute-start | bytes 1592 | tf_op jit(solution)/shard_map/ppermute | solution.py:21
  670.8 10.5 %copy-start = (f32[2,64,128]{2,1,0:T(8,128)}, f32[2,64,128]{2,1,0:T(8,128)S(1)}, u32[]{:S(2)}) copy-start(f32[2,64,128]{2,1,0:T(8,128)S(1)} %multiply_add_fusion) | copy-start | bytes 196612
  670.8 10.4 %collective-permute-start.17 = (f32[2,1,128]{2,1,0:T(1,128)S(1)}, f32[2,1,128]{2,1,0:T(1,128)S(1)}, u32[]{:S(2)}, u32[]{:S(2)}) collective-permute-start(f32[2,1,128]{2,1,0:T(1,128)S(1)} %slice.398), channel_id=1, source_target_pairs={{32,0},{64,32},{96,64},{128,96},{160,128},{192,160},{224,192},{256... | collective-permute-start | bytes 3080 | tf_op jit(solution)/shard_map/ppermute | solution.py:33
  672.7 8.5 %collective-permute-start.16 = (f32[2,64,1]{2,1,0:T(8,128)S(1)}, f32[2,64,1]{2,1,0:T(8,128)S(1)}, u32[]{:S(2)}, u32[]{:S(2)}) collective-permute-start(f32[2,64,1]{2,1,0:T(8,128)S(1)} %bitcast.19), channel_id=1, source_target_pairs={{1,0},{2,1},{3,2},{4,3},{5,4},{6,5},{7,6},{8,7},{9,8},{10,9},{11,1... | collective-permute-start | bytes 1544 | tf_op jit(solution)/shard_map/ppermute | solution.py:33
  (1 other events, 0.8 us)
